TPU v7x, 512 devices: a whole 4x4x16 slice. The times are simulated.
512 devices in a mesh: ctx: 16 (over y, z_hi), exp: 16 (over x, z_lo), dp: 2 (over core).
Axes of the slice: x: 4, y: 4, z: 16 (z_hi: 4, z_lo: 4; z = z_hi * 4 + z_lo), core: 2. Of those that a mesh axis runs over, the one named last changes fastest.
Arguments:
- queries: bfloat16 [32, 3072, 2048], P(('dp', 'exp'), 'ctx'), parts along dimension 0, may hold values from -38 to 38
- keys: bfloat16 [32, 3072, 256], P(('dp', 'exp'), 'ctx'), parts along dimension 0, may hold values from -4 to 4
- values: bfloat16 [32, 3072, 256], P(('dp', 'exp'), 'ctx'), parts along dimension 0, may hold values from -6 to 6
- segments: int32 [32, 3072], P(('dp', 'exp')), parts along dimension 0, may hold values from 0 to 7, never falling along the last dimension, each value on 1 to 1536 neighbouring positions
- residual: bfloat16 [32, 3072, 1024], P(('dp', 'exp'), 'ctx'), parts along dimension 0, may hold values from -3 to 3
- out_weight: bfloat16 [2048, 1024], P('ctx'), may hold values from -0.125 to 0.125
- gain: float32 [1024], replicated, may hold values from 0.1 to 1.9
- expert_ids: int32 [32, 3072, 8], P(('dp', 'exp'), 'ctx'), parts along dimension 0, may hold values from 0 to 127, all different within a row; in each aligned block of 192 rows (0 to 191, 192 to 383, ..., all dimensions but the last counted through in order) at most 24 rows name the same one
- route_weights: float32 [32, 3072, 8], P(('dp', 'exp'), 'ctx'), parts along dimension 0, may hold values from 0.05 to 0.5
- w_gate: bfloat16 [16, 1024, 384], P('exp'), may hold values from -0.1875 to 0.1875
- w_up: bfloat16 [16, 1024, 384], P('exp'), may hold values from -0.1875 to 0.1875
- w_down: bfloat16 [16, 384, 1024], P('exp'), may hold values from -0.3125 to 0.3125
Outputs:
- layer_out: bfloat16 [32, 3072, 1024], P(('dp', 'exp'), 'ctx'), parts along dimension 0
There are 2 independent parts, one for each index of `dp`. A program takes and returns all parts, laid end to end along the dimension named above; an argument that names none is the same for every part. Nothing has to cross between parts.
Inputs may be any that keep to these rules, and one draw needn't show every extreme that they name: `expert_ids`: in every aligned block of 192 positions of a sequence (one slab), no expert is named by more than 24 tokens, and in every draw some expert is named by exactly 24 tokens of some block; a token names 8 different experts. `segments`: document numbers never fall along a sequence.
All inputs are finite; a program needn't handle non-finite values.
Results may differ from a plain program's by a relative error of at most 0.006.
Values may be sent and summed in bfloat16 or wider, within the bound.
A program may use at most 64 MiB of HBM per device.

v0:
```python
import math

import jax
import jax.numpy as jnp
from jax import lax
from jax.sharding import PartitionSpec as P

HQ = 16
KVH = 2
HD = 128
TOP = 8
CAP = 24


def per_device(
    queries,
    keys,
    values,
    segments,
    residual,
    out_weight,
    gain,
    expert_ids,
    route_weights,
    w_gate,
    w_up,
    w_down,
):
    tok_rows = queries.shape[1]
    model_width = residual.shape[2]
    groups = HQ // KVH
    scale_factor = 1.0 / math.sqrt(HD)
    rank_ctx = lax.axis_index("ctx")
    query_pos = rank_ctx * tok_rows + jnp.arange(tok_rows, dtype=jnp.int32)
    seg_line = segments[0]
    query_seg = lax.dynamic_slice_in_dim(seg_line, rank_ctx * tok_rows, tok_rows)
    query_heads = queries[0].reshape(tok_rows, KVH, groups, HD)

    def attend_block(running, inputs):
        key_blk, value_blk, blk_start = inputs
        blk_rows = key_blk.shape[0]
        key_pos = blk_start + jnp.arange(blk_rows, dtype=jnp.int32)
        key_seg = lax.dynamic_slice_in_dim(seg_line, blk_start, blk_rows)
        run_max, run_sum, accum = running
        scores = (
            jnp.einsum("qkgd,skd->qkgs", query_heads, key_blk, preferred_element_type=jnp.float32)
            * scale_factor
        )
        allowed = (
            (key_pos[None, :] <= query_pos[:, None]) & (key_seg[None, :] == query_seg[:, None])
        )[:, None, None, :]
        masked_scores = jnp.where(allowed, scores, -1e30)
        new_max = jnp.maximum(run_max, jnp.max(masked_scores, axis=-1))
        correction = jnp.exp(run_max - new_max)
        expo = jnp.where(allowed, jnp.exp(scores - new_max[..., None]), 0.0)
        new_sum = run_sum * correction + jnp.sum(expo, axis=-1)
        probs = expo.astype(jnp.bfloat16)
        new_accum = accum * correction[..., None] + jnp.einsum(
            "qkgs,skd->qkgd", probs, value_blk, preferred_element_type=jnp.float32
        )
        updated = (new_max, new_sum, new_accum)
        return (updated, None)

    initial = (
        jnp.full((tok_rows, KVH, groups), -1e30, jnp.float32),
        jnp.zeros((tok_rows, KVH, groups), jnp.float32),
        jnp.zeros((tok_rows, KVH, groups, HD), jnp.float32),
    )
    running = initial
    key_piece = lax.all_gather(keys, "ctx", axis=1, tiled=True)
    value_piece = lax.all_gather(values, "ctx", axis=1, tiled=True)
    row_count = key_piece.shape[1]
    blk_rows = math.gcd(row_count, 512)
    blk_count = row_count // blk_rows
    key_blocks = key_piece[0].reshape(blk_count, blk_rows, KVH, HD)
    value_blocks = value_piece[0].reshape(blk_count, blk_rows, KVH, HD)
    blk_starts = blk_rows * jnp.arange(blk_count, dtype=jnp.int32)
    running, _ = lax.scan(attend_block, running, (key_blocks, value_blocks, blk_starts))
    run_max, run_sum, accum = running
    attended = (accum / run_sum[..., None]).reshape(tok_rows, HQ * HD).astype(jnp.bfloat16)
    projected = jnp.dot(
        attended,
        lax.all_gather(out_weight, "ctx", axis=0, tiled=True),
        preferred_element_type=jnp.float32,
    )
    hidden_state = residual[0].astype(jnp.float32) + projected
    normed = (
        hidden_state
        * lax.rsqrt(jnp.mean(hidden_state * hidden_state, axis=-1, keepdims=True) + 1e-06)
        * gain
    ).astype(jnp.bfloat16)
    owners = lax.axis_size("exp")
    chosen = expert_ids[0]
    active = chosen < owners
    owner_range = jnp.arange(owners, dtype=jnp.int32)
    hit_table = (
        ((chosen[:, :, None] == owner_range) & active[:, :, None])
        .astype(jnp.int32)
        .reshape(tok_rows * TOP, owners)
    )
    rank_in = jnp.sum((jnp.cumsum(hit_table, axis=0) - 1) * hit_table, axis=1).reshape(
        tok_rows, TOP
    )
    slot_total = owners * CAP
    slot_of = jnp.where(active, chosen * CAP + rank_in, slot_total)
    slot_range = jnp.arange(slot_total, dtype=jnp.int32)
    placing = jnp.any(slot_of[None, :, :] == slot_range[:, None, None], axis=2).astype(jnp.bfloat16)
    outgoing = (
        jnp.dot(placing, normed, preferred_element_type=jnp.float32)
        .astype(jnp.bfloat16)
        .reshape(owners, CAP, model_width)
    )
    arrived = lax.all_to_all(outgoing, "exp", split_axis=0, concat_axis=0, tiled=True)
    item_count = arrived.shape[1]
    flat_rows = arrived.reshape(owners * item_count, model_width)
    gate_part = jnp.dot(flat_rows, w_gate[0], preferred_element_type=jnp.float32)
    up_part = jnp.dot(flat_rows, w_up[0], preferred_element_type=jnp.float32)
    expert_hidden = (jax.nn.silu(gate_part) * up_part).astype(jnp.bfloat16)
    expert_out = jnp.dot(expert_hidden, w_down[0], preferred_element_type=jnp.float32).astype(
        jnp.bfloat16
    )
    returned = lax.all_to_all(
        expert_out.reshape(owners, item_count, model_width),
        "exp",
        split_axis=0,
        concat_axis=0,
        tiled=True,
    )
    padded_back = jnp.concatenate(
        [returned.reshape(slot_total, model_width), jnp.zeros((1, model_width), jnp.bfloat16)],
        axis=0,
    )
    picked = padded_back[slot_of]
    mix_weights = jnp.where(active, route_weights[0], 0.0)
    moe_sum = jnp.einsum("tk,tkd->td", mix_weights, picked.astype(jnp.float32))
    layer_out = (hidden_state + moe_sum).astype(jnp.bfloat16)
    return layer_out[None]


def solution(mesh):
    return jax.shard_map(
        per_device,
        mesh=mesh,
        in_specs=(
            P(("dp", "exp"), "ctx", None),
            P(("dp", "exp"), "ctx", None),
            P(("dp", "exp"), "ctx", None),
            P(("dp", "exp"), None),
            P(("dp", "exp"), "ctx", None),
            P("ctx", None),
            P(),
            P(("dp", "exp"), "ctx", None),
            P(("dp", "exp"), "ctx", None),
            P("exp", None, None),
            P("exp", None, None),
            P("exp", None, None),
        ),
        out_specs=P(("dp", "exp"), "ctx", None),
        check_vma=False,
    )
```

profile of v0, /device:TPU:1, one launch (start us, length us, event | category | flops | bytes accessed | tf_op | source)
XLA Modules:
  0.0 393.0 jit_solution(8537777085268056994)
XLA Ops:
  10.4 4.5 %reduce-window.6 = s32[16,12,128]{2,1,0:T(8,128)S(1)} reduce-window(s32[16,12,128]{2,1,0:T(8,128)S(1)} %fusion.41, s32[]{:T(128)} %constant.11.clone.1), window={size=1x1x128 pad=0_0x0_0x127_0}, to_apply=%region_4.5 | reduce-window | flops 3121152 | bytes 196612 | tf_op jit(solution)/shard_map/reduce-window
  20.8 79.8 %all-gather.6.cloned.1.call-done = bf16[1,3072,256]{2,1,0:T(8,128)(2,1)} async-done(((bf16[1,192,256]{2,1,0:T(8,128)(2,1)}), bf16[1,3072,256]{2,1,0:T(8,128)(2,1)}) %all-gather.6.cloned.1.call-update) | async-done | bytes 1572880 | tf_op jit(solution)/shard_map/all_gather | solution.py:71
  103.0 81.9 %all-gather.4.cloned.1.call-done = bf16[1,3072,256]{2,1,0:T(8,128)(2,1)} async-done(((bf16[1,192,256]{2,1,0:T(8,128)(2,1)}), bf16[1,3072,256]{2,1,0:T(8,128)(2,1)}) %all-gather.4.cloned.1.call-update) | async-done | bytes 1572880 | tf_op jit(solution)/shard_map/all_gather | solution.py:70
  188.3 116.4 %while.15 = (s32[]{:T(128)}, f32[192,2,8]{0,2,1:T(8,128)S(1)}, f32[192,2,8]{0,2,1:T(8,128)S(1)}, f32[192,2,8,128]{3,0,2,1:T(8,128)}, s32[6]{0:T(128)}, /*index=5...) while((s32[]{:T(128)}, f32[192,2,8]{0,2,1:T(8,128)S(1)}, ...), condition=%wide.region_3.4_spmd.clone, body=%wide.region_0.3_spmd.clone.sunk | while | flops 824098496 | bytes 50147816 | solution.py:78
  198.7 4.3 %fusion.61 = f32[192,2,8]{0,2,1:T(8,128)S(1)} fusion(f32[2,512,192,8]{1,2,3,0:T(8,128)} %get-tuple-element.231, f32[192,2,8]{0,2,1:T(8,128)S(1)} %select_maximum_fusion.2, pred[192,512]{1,0:T(8,128)(4,1)S(1)} %compare_and_fusion.2), kind=kLoop, calls=%fused_computation.8.clone.1 | loop fusion | flops 6288384 | bytes 6414336 | tf_op jit(solution)/shard_map/while/body/eval_jaxpr/reduce_sum | solution.py:56
  213.3 3.7 fusion.60
  217.1 4.3 %fusion.61 = f32[192,2,8]{0,2,1:T(8,128)S(1)} fusion(f32[2,512,192,8]{1,2,3,0:T(8,128)} %get-tuple-element.231, f32[192,2,8]{0,2,1:T(8,128)S(1)} %select_maximum_fusion.2, pred[192,512]{1,0:T(8,128)(4,1)S(1)} %compare_and_fusion.2), kind=kLoop, calls=%fused_computation.8.clone.1 | loop fusion | flops 6288384 | bytes 6414336 | tf_op jit(solution)/shard_map/while/body/eval_jaxpr/reduce_sum | solution.py:56
  221.7 4.5 %bitcast_add_fusion.4 = f32[192,2,8,128]{3,0,2,1:T(8,128)} fusion(f32[192,2,8,128]{3,0,2,1:T(8,128)} %get-tuple-element.252, f32[2,512,192,8]{1,2,3,0:T(8,128)S(1)} %copy-done.1, f32[192,2,8]{0,2,1:T(8,128)S(1)} %select_maximum_fusion.2, pred[192,512]{1,0:T(8,128)(4,1)S(1)} %compare_and_fusion.2, f32[192,2,8]{0,2,1:T(8,128)S(1)} %get-tuple-element.233, ...), kind=kOutput, calls=%fused_computation.14.clone.1 | convolution fusion | flops 410124288 | bytes 9822209 | tf_op jit(solution)/shard_map/while/body/eval_jaxpr/qkgs,skd->qkgd/dot_general | solution.py:58
  232.9 3.7 fusion.60
  236.7 4.3 %fusion.61 = f32[192,2,8]{0,2,1:T(8,128)S(1)} fusion(f32[2,512,192,8]{1,2,3,0:T(8,128)} %get-tuple-element.231, f32[192,2,8]{0,2,1:T(8,128)S(1)} %select_maximum_fusion.2, pred[192,512]{1,0:T(8,128)(4,1)S(1)} %compare_and_fusion.2), kind=kLoop, calls=%fused_computation.8.clone.1 | loop fusion | flops 6288384 | bytes 6414336 | tf_op jit(solution)/shard_map/while/body/eval_jaxpr/reduce_sum | solution.py:56
  241.3 4.7 %bitcast_add_fusion.4 = f32[192,2,8,128]{3,0,2,1:T(8,128)} fusion(f32[192,2,8,128]{3,0,2,1:T(8,128)} %get-tuple-element.252, f32[2,512,192,8]{1,2,3,0:T(8,128)S(1)} %copy-done.1, f32[192,2,8]{0,2,1:T(8,128)S(1)} %select_maximum_fusion.2, pred[192,512]{1,0:T(8,128)(4,1)S(1)} %compare_and_fusion.2, f32[192,2,8]{0,2,1:T(8,128)S(1)} %get-tuple-element.233, ...), kind=kOutput, calls=%fused_computation.14.clone.1 | convolution fusion | flops 410124288 | bytes 9822209 | tf_op jit(solution)/shard_map/while/body/eval_jaxpr/qkgs,skd->qkgd/dot_general | solution.py:58
  252.6 3.7 fusion.60
  256.4 4.3 %fusion.61 = f32[192,2,8]{0,2,1:T(8,128)S(1)} fusion(f32[2,512,192,8]{1,2,3,0:T(8,128)} %get-tuple-element.231, f32[192,2,8]{0,2,1:T(8,128)S(1)} %select_maximum_fusion.2, pred[192,512]{1,0:T(8,128)(4,1)S(1)} %compare_and_fusion.2), kind=kLoop, calls=%fused_computation.8.clone.1 | loop fusion | flops 6288384 | bytes 6414336 | tf_op jit(solution)/shard_map/while/body/eval_jaxpr/reduce_sum | solution.py:56
  261.0 4.5 %bitcast_add_fusion.4 = f32[192,2,8,128]{3,0,2,1:T(8,128)} fusion(f32[192,2,8,128]{3,0,2,1:T(8,128)} %get-tuple-element.252, f32[2,512,192,8]{1,2,3,0:T(8,128)S(1)} %copy-done.1, f32[192,2,8]{0,2,1:T(8,128)S(1)} %select_maximum_fusion.2, pred[192,512]{1,0:T(8,128)(4,1)S(1)} %compare_and_fusion.2, f32[192,2,8]{0,2,1:T(8,128)S(1)} %get-tuple-element.233, ...), kind=kOutput, calls=%fused_computation.14.clone.1 | convolution fusion | flops 410124288 | bytes 9822209 | tf_op jit(solution)/shard_map/while/body/eval_jaxpr/qkgs,skd->qkgd/dot_general | solution.py:58
  272.2 3.7 fusion.60
  275.9 4.3 %fusion.61 = f32[192,2,8]{0,2,1:T(8,128)S(1)} fusion(f32[2,512,192,8]{1,2,3,0:T(8,128)} %get-tuple-element.231, f32[192,2,8]{0,2,1:T(8,128)S(1)} %select_maximum_fusion.2, pred[192,512]{1,0:T(8,128)(4,1)S(1)} %compare_and_fusion.2), kind=kLoop, calls=%fused_computation.8.clone.1 | loop fusion | flops 6288384 | bytes 6414336 | tf_op jit(solution)/shard_map/while/body/eval_jaxpr/reduce_sum | solution.py:56
  280.7 4.5 %bitcast_add_fusion.4 = f32[192,2,8,128]{3,0,2,1:T(8,128)} fusion(f32[192,2,8,128]{3,0,2,1:T(8,128)} %get-tuple-element.252, f32[2,512,192,8]{1,2,3,0:T(8,128)S(1)} %copy-done.1, f32[192,2,8]{0,2,1:T(8,128)S(1)} %select_maximum_fusion.2, pred[192,512]{1,0:T(8,128)(4,1)S(1)} %compare_and_fusion.2, f32[192,2,8]{0,2,1:T(8,128)S(1)} %get-tuple-element.233, ...), kind=kOutput, calls=%fused_computation.14.clone.1 | convolution fusion | flops 410124288 | bytes 9822209 | tf_op jit(solution)/shard_map/while/body/eval_jaxpr/qkgs,skd->qkgd/dot_general | solution.py:58
  291.8 3.7 fusion.60
  295.6 4.3 %fusion.61 = f32[192,2,8]{0,2,1:T(8,128)S(1)} fusion(f32[2,512,192,8]{1,2,3,0:T(8,128)} %get-tuple-element.231, f32[192,2,8]{0,2,1:T(8,128)S(1)} %select_maximum_fusion.2, pred[192,512]{1,0:T(8,128)(4,1)S(1)} %compare_and_fusion.2), kind=kLoop, calls=%fused_computation.8.clone.1 | loop fusion | flops 6288384 | bytes 6414336 | tf_op jit(solution)/shard_map/while/body/eval_jaxpr/reduce_sum | solution.py:56
  300.2 4.5 %bitcast_add_fusion.4 = f32[192,2,8,128]{3,0,2,1:T(8,128)} fusion(f32[192,2,8,128]{3,0,2,1:T(8,128)} %get-tuple-element.252, f32[2,512,192,8]{1,2,3,0:T(8,128)S(1)} %copy-done.1, f32[192,2,8]{0,2,1:T(8,128)S(1)} %select_maximum_fusion.2, pred[192,512]{1,0:T(8,128)(4,1)S(1)} %compare_and_fusion.2, f32[192,2,8]{0,2,1:T(8,128)S(1)} %get-tuple-element.233, ...), kind=kOutput, calls=%fused_computation.14.clone.1 | convolution fusion | flops 410124288 | bytes 9822209 | tf_op jit(solution)/shard_map/while/body/eval_jaxpr/qkgs,skd->qkgd/dot_general | solution.py:58
  307.2 11.3 %all-gather.8.cloned.1.call-done = bf16[2048,1024]{1,0:T(8,128)(2,1)} async-done(((bf16[128,1024]{1,0:T(8,128)(2,1)}), bf16[2048,1024]{1,0:T(8,128)(2,1)}) %all-gather.8.cloned.1.call-update) | async-done | bytes 4194320 | tf_op jit(solution)/shard_map/all_gather | solution.py:83
  322.3 25.8 %all_to_all.10 = bf16[16,24,1024]{2,1,0:T(8,128)(2,1)S(1)} all-to-all(bf16[16,24,1024]{2,1,0:T(8,128)(2,1)S(1)} %bitcast.127), channel_id=1, replica_groups=mesh['ctx'=16,'exp'=16,'dp'=2] {'exp'}, dimensions={0} | all-to-all | bytes 1572864 | tf_op jit(solution)/shard_map/all_to_all | solution.py:113
  355.9 20.9 %all-to-all-done.1 = bf16[16,24,1024]{2,1,0:T(8,128)(2,1)S(1)} async-done(((bf16[16,24,1024]{2,1,0:T(8,128)(2,1)}), bf16[16,24,1024]{2,1,0:T(8,128)(2,1)S(1)}, u32[]{:S(2)}, u32[]{:S(2)}) %all-to-all-start.1) | async-done | bytes 786464 | tf_op jit(solution)/shard_map/all_to_all | solution.py:122
  376.9 5.8 %gather_fusion = bf16[1536,1024]{1,0:T(8,128)(2,1)} fusion(bf16[385,1024]{1,0:T(8,128)(2,1)S(1)} %concatenate.3, s32[2048]{0:T(1024)S(1)} %pad_clamp_fusion), kind=kCustom, calls=%fused_computation | custom fusion | bytes 6297600 | tf_op jit(solution)/shard_map/gather | solution.py:133
  (133 shorter events, 70.8 us)
Async XLA Ops:
  6.5 342.2 %copy-start = (bf16[1,384,1024]{2,1,0:T(8,128)(2,1)S(1)}, bf16[1,384,1024]{2,1,0:T(8,128)(2,1)}, u32[]{:S(2)}) copy-start(bf16[1,384,1024]{2,1,0:T(8,128)(2,1)} %param.25) | copy-start | bytes 2359300
  6.5 94.1 %all-gather.6.cloned.1.call-start = ((), (), s32[]{:S(2)}) async-start(), calls=%async_computation.3 | async-start | bytes 1671168 | tf_op jit(solution)/shard_map/all_gather | solution.py:71
  7.3 177.6 %all-gather.4.cloned.1.call-start = ((), (), s32[]{:S(2)}) async-start(), calls=%async_computation.2 | async-start | bytes 1671168 | tf_op jit(solution)/shard_map/all_gather | solution.py:70
  8.0 310.5 %all-gather.8.cloned.1.call-start = ((), (), s32[]{:S(2)}) async-start(), calls=%async_computation.4 | async-start | bytes 4456448 | tf_op jit(solution)/shard_map/all_gather | solution.py:83
  9.6 9.6 %copy-start.2 = (s32[1,192,8]{2,1,0:T(8,128)}, s32[1,192,8]{2,1,0:T(8,128)S(1)}, u32[]{:S(2)}) copy-start(s32[1,192,8]{2,1,0:T(8,128)S(1)} %copy.27) | copy-start | bytes 18436
  15.7 0.6 copy-start.6
  198.7 4.9 %copy-start.1 = (f32[2,512,192,8]{1,2,3,0:T(8,128)S(1)}, f32[2,512,192,8]{1,2,3,0:T(8,128)}, u32[]{:S(2)}) copy-start(f32[2,512,192,8]{1,2,3,0:T(8,128)} %get-tuple-element.231) | copy-start | bytes 18874372 | tf_op jit(solution)/shard_map/while
  217.1 4.7 %copy-start.1 = (f32[2,512,192,8]{1,2,3,0:T(8,128)S(1)}, f32[2,512,192,8]{1,2,3,0:T(8,128)}, u32[]{:S(2)}) copy-start(f32[2,512,192,8]{1,2,3,0:T(8,128)} %get-tuple-element.231) | copy-start | bytes 18874372 | tf_op jit(solution)/shard_map/while
  236.7 4.6 %copy-start.1 = (f32[2,512,192,8]{1,2,3,0:T(8,128)S(1)}, f32[2,512,192,8]{1,2,3,0:T(8,128)}, u32[]{:S(2)}) copy-start(f32[2,512,192,8]{1,2,3,0:T(8,128)} %get-tuple-element.231) | copy-start | bytes 18874372 | tf_op jit(solution)/shard_map/while
  256.4 4.6 %copy-start.1 = (f32[2,512,192,8]{1,2,3,0:T(8,128)S(1)}, f32[2,512,192,8]{1,2,3,0:T(8,128)}, u32[]{:S(2)}) copy-start(f32[2,512,192,8]{1,2,3,0:T(8,128)} %get-tuple-element.231) | copy-start | bytes 18874372 | tf_op jit(solution)/shard_map/while
  275.9 4.7 %copy-start.1 = (f32[2,512,192,8]{1,2,3,0:T(8,128)S(1)}, f32[2,512,192,8]{1,2,3,0:T(8,128)}, u32[]{:S(2)}) copy-start(f32[2,512,192,8]{1,2,3,0:T(8,128)} %get-tuple-element.231) | copy-start | bytes 18874372 | tf_op jit(solution)/shard_map/while
  295.6 4.6 %copy-start.1 = (f32[2,512,192,8]{1,2,3,0:T(8,128)S(1)}, f32[2,512,192,8]{1,2,3,0:T(8,128)}, u32[]{:S(2)}) copy-start(f32[2,512,192,8]{1,2,3,0:T(8,128)} %get-tuple-element.231) | copy-start | bytes 18874372 | tf_op jit(solution)/shard_map/while
  304.8 13.8 %copy-start.10 = (bf16[1,192,1024]{2,1,0:T(8,128)(2,1)S(1)}, bf16[1,192,1024]{2,1,0:T(8,128)(2,1)}, u32[]{:S(2)}) copy-start(bf16[1,192,1024]{2,1,0:T(8,128)(2,1)} %param.18) | copy-start | bytes 1179652
  318.5 3.3 copy-start.5
  318.5 3.3 copy-start.9
  321.8 26.3 %copy-start.4 = (bf16[1,1024,384]{2,1,0:T(8,128)(2,1)S(1)}, bf16[1,1024,384]{2,1,0:T(8,128)(2,1)}, u32[]{:S(2)}) copy-start(bf16[1,1024,384]{2,1,0:T(8,128)(2,1)} %param.23) | copy-start | bytes 2359300
  348.7 6.7 %copy-start.7 = (s32[1536]{0:T(1024)S(1)}, s32[1536]{0:T(1024)}, u32[]{:S(2)}) copy-start(s32[1536]{0:T(1024)} %copy-done.6) | copy-start | bytes 18436
  348.7 6.9 %copy-start.3 = (s32[1,192,8]{2,1,0:T(8,128)S(1)}, s32[1,192,8]{2,1,0:T(8,128)}, u32[]{:S(2)}) copy-start(s32[1,192,8]{2,1,0:T(8,128)} %copy-done.2) | copy-start | bytes 18436
  348.7 7.0 %copy-start.8 = (f32[1,192,8]{1,2,0:T(8,128)S(1)}, f32[1,192,8]{1,2,0:T(8,128)}, u32[]{:S(2)}) copy-start(f32[1,192,8]{1,2,0:T(8,128)} %param.22) | copy-start | bytes 18436
  351.8 25.0 %all-to-all-start.1 = ((bf16[16,24,1024]{2,1,0:T(8,128)(2,1)}), bf16[16,24,1024]{2,1,0:T(8,128)(2,1)S(1)}, u32[]{:S(2)}, u32[]{:S(2)}) async-start(bf16[16,24,1024]{2,1,0:T(8,128)(2,1)} %bitcast.13), calls=%async_computation.1 | async-start | bytes 1572864 | tf_op jit(solution)/shard_map/all_to_all | solution.py:122
Sparse Core Ops, SparseCore 0:
  10.4 90.1 all-gather.5
  103.7 81.1 all-gather.3
  187.9 130.5 all-gather.7
where the time goes:
time: 395 us; the launch traced here: 393 us
  waiting for transfers between devices  196 us (50%)
  matrix products  58.6 us (15%)
  other arithmetic  44.6 us (11%)
  local copies, waits for them, and re-layouts  39.7 us (10%)
  blocking collectives  25.8 us (7%)
  between operations  13.4 us (3%)
  loops' own time  11.2 us (3%)
    all_gather x1, waiting for transfers between devices, per_device(): key_piece = lax.all_gather(keys, 'ctx', axis=1, tiled=True)  81.9 us
    all_gather x1, waiting for transfers between devices, per_device(): value_piece = lax.all_gather(values, 'ctx', axis=1, tiled=True)  79.8 us
    reduce_sum x6, other arithmetic, attend_block(): new_sum = run_sum * correction + jnp.sum(expo, axis=-1)  26 us
    dot_general x6, matrix products, attend_block(): jnp.einsum('qkgs,skd->qkgd', probs, value_blk, preferred_element_type=jnp...  25.9 us
    all_to_all x1, blocking collectives, per_device(): lax.all_to_all(outgoing, 'exp', split_axis=0, concat_axis=0, tiled=True)  25.8 us
    dot_general x6, matrix products, attend_block(): jnp.einsum('qkgd,skd->qkgs', query_heads, key_blk, preferred_element_type...  22.4 us
    all_to_all x1, waiting for transfers between devices, per_device(): lax.all_to_all(expert_out.reshape(owners, item_count, model_width), 'exp'...  20.9 us
    dynamic_slice x12, local copies, waits for them, and re-layouts, per_device(): lax.scan(attend_block, running, (key_blocks, value_blocks, blk_starts))  15.4 us
  transfers between devices with their start and end apart: 4, of which 4 were waited for; matrix products, arithmetic and copies ran while one was open for 31% of the time, Pallas kernels for 0%

commit v1 on v0

v1 whole, which is shorter than its diff:
```python
import math

import jax
import jax.numpy as jnp
from jax import lax
from jax.experimental import pallas as pl
from jax.experimental.pallas import tpu as pltpu
from jax.sharding import PartitionSpec as P

HQ = 16
KVH = 2
HD = 128
TOP = 8
CAP = 24
TOK = 192
WIDTH = 1024
OWNERS = 16
SLOTS = OWNERS * CAP
PER = 4
BLOCKS = HQ // PER
LANES = PER * TOK
NEG = -1e30
MESH = pl.DeviceIdType.MESH
SCALE2 = math.log2(math.e) / math.sqrt(HD)
OWN, LEFT, RIGHT, FAR = range(4)


def attend_kernel(
    queries, segs, residual, gain, ids, weights, keys_hbm, values_hbm, w_hbm,
    hidden_out, rows_out, hi_out, lo_out,
    kbuf, vbuf, vtransit, wbuf, q_s, m_s, l_s, acc_s, start_s, qpos_s, att_s,
    send_sems, recv_sems, local_sems,
):
    c = lax.axis_index("ctx")
    e = lax.axis_index("exp")
    core = lax.axis_index("dp")
    y, h = c // 4, c % 4
    x, z = e // 4, e % 4
    zr, zl = {"ctx": y * 4 + (h + 1) % 4}, {"ctx": y * 4 + (h + 3) % 4}
    yu, yd = {"ctx": ((y + 1) % 4) * 4 + h}, {"ctx": ((y + 3) % 4) * 4 + h}
    xu, xd = {"exp": ((x + 1) % 4) * 4 + z}, {"exp": ((x + 3) % 4) * 4 + z}
    twin = {"dp": 1 - core}
    partners = (zr, zl, yu, yd, xu, xd, twin)
    at = (h, (h + 3) % 4, (h + 1) % 4, (h + 2) % 4)

    sends = []
    recv_index = {}

    def recv_sem(name):
        return recv_sems.at[recv_index.setdefault(name, len(recv_index))]

    def send(src, dst, name, to):
        copy = pltpu.make_async_remote_copy(
            src_ref=src, dst_ref=dst, send_sem=send_sems.at[len(sends)], recv_sem=recv_sem(name),
            device_id=to, device_id_type=MESH,
        )
        copy.start()
        sends.append(copy)

    def arrived(dst, name):
        pltpu.make_async_remote_copy(
            src_ref=dst, dst_ref=dst, send_sem=send_sems.at[0], recv_sem=recv_sem(name),
            device_id=twin, device_id_type=MESH,
        ).wait_recv()

    barrier = pltpu.get_barrier_semaphore()
    for partner in partners:
        pl.semaphore_signal(barrier, inc=1, device_id=partner, device_id_type=MESH)
    own_k = pltpu.make_async_copy(keys_hbm.at[0], kbuf.at[0, h], local_sems.at[0])
    own_v = pltpu.make_async_copy(values_hbm.at[0], vbuf.at[0, h], local_sems.at[1])
    piece = pl.multiple_of(x * 32 + core * 16, 16)
    w_own = w_hbm.at[pl.ds(piece, 16), :]
    own_w = pltpu.make_async_copy(w_own, wbuf.at[c, pl.ds(piece, 16), :], local_sems.at[2])
    own_k.start()
    own_v.start()
    own_w.start()
    pl.semaphore_wait(barrier, len(partners))

    k_own, v_own = keys_hbm.at[0], values_hbm.at[0]

    def w_at(shard, half=None):
        if half is None:
            return wbuf.at[shard, pl.ds(piece, 16), :]
        return wbuf.at[shard, pl.ds(piece, 16), pl.ds(half * 512, 512)]

    send(w_own, w_at(c), "wz-left", zr)
    send(w_own, w_at(c), "wz-right", zl)
    send(k_own, kbuf.at[0, h], ("k", 0, LEFT), zr)
    send(k_own, kbuf.at[0, h], ("k", 0, RIGHT), zl)
    send(k_own, kbuf.at[1, h], ("k", 1, OWN), yu)
    send(v_own, vbuf.at[1, h], ("v", 1, OWN), yu)
    send(v_own, vtransit.at[h], ("t", OWN), yd)

    for head in range(HQ):
        q_s[head // PER, (head % PER) * TOK:(head % PER + 1) * TOK, :] = (
            queries[:, head * HD:(head + 1) * HD]
        )
    line = segs[...]
    mine = jnp.zeros((1, TOK), jnp.int32)
    for slab in range(16):
        mine = jnp.where(c == slab, line[:, slab * TOK:(slab + 1) * TOK], mine)
    start = jnp.zeros((1, TOK), jnp.int32)
    for doc in range(1, 8):
        count = jnp.sum((line < doc).astype(jnp.int32), axis=1, keepdims=True)
        start = jnp.where(mine == doc, count, start)
    start_s[...] = jnp.concatenate([start] * PER, axis=1)
    qpos = c * TOK + lax.broadcasted_iota(jnp.int32, (1, TOK), 1)
    qpos_s[...] = jnp.concatenate([qpos] * PER, axis=1)

    def attend(r, hh, diagonal):
        first = ((y - r) * 4 + hh) * TOK

        def block(b, carry):
            lane = pl.multiple_of((b // (BLOCKS // KVH)) * HD, HD)
            k = kbuf[r, hh, :, pl.ds(lane, HD)]
            v = vbuf[r, hh, :, pl.ds(lane, HD)]
            s = lax.dot_general(
                k, q_s[b], (((1,), (1,)), ((), ())), preferred_element_type=jnp.float32
            )
            kpos = first + lax.broadcasted_iota(jnp.int32, (TOK, LANES), 0)
            ok = kpos >= start_s[...]
            if diagonal:
                ok = ok & (kpos <= qpos_s[...])
            s = jnp.where(ok, s, NEG)
            top = jnp.max(s, axis=0, keepdims=True)
            if diagonal:
                m = top
            else:
                old = m_s[b]
                m = jnp.maximum(old, top)
                alpha = jnp.exp2((old - m) * SCALE2)
            p = jnp.exp2((s - m) * SCALE2)
            total = jnp.sum(p, axis=0, keepdims=True)
            mixed = lax.dot_general(
                v, p.astype(jnp.bfloat16), (((0,), (0,)), ((), ())),
                preferred_element_type=jnp.float32,
            )
            m_s[b] = m
            if diagonal:
                l_s[b] = total
                acc_s[b] = mixed
            else:
                l_s[b] = l_s[b] * alpha + total
                acc_s[b] = acc_s[b] * alpha + mixed
            return carry

        lax.fori_loop(0, BLOCKS, block, 0)

    def same_row(g):
        hh = at[g]
        arrived(kbuf.at[0, hh], ("k", 0, g))
        if g == LEFT:
            send(kbuf.at[0, hh], kbuf.at[0, hh], ("k", 0, FAR), zr)
        send(kbuf.at[0, hh], kbuf.at[1, hh], ("k", 1, g), yu)
        arrived(vbuf.at[0, hh], ("v", 0, g))
        if g == RIGHT:
            send(vbuf.at[0, hh], vbuf.at[0, hh], ("v", 0, FAR), zl)
        send(vbuf.at[0, hh], vbuf.at[1, hh], ("v", 1, g), yu)
        send(vbuf.at[0, hh], vtransit.at[hh], ("t", g), yd)

        @pl.when(hh < h)
        def _():
            attend(0, hh, False)

    def next_row(g):
        hh = at[g]
        arrived(kbuf.at[1, hh], ("k", 1, g))
        send(kbuf.at[1, hh], kbuf.at[2, hh], ("k", 2, g), yu)
        arrived(vtransit.at[hh], ("t", g))
        send(vtransit.at[hh], vbuf.at[2, hh], ("v", 2, g), yd)
        arrived(vbuf.at[1, hh], ("v", 1, g))

        @pl.when(y >= 1)
        def _():
            attend(1, hh, False)

    def last_row(g):
        hh = at[g]
        arrived(kbuf.at[2, hh], ("k", 2, g))
        arrived(vbuf.at[2, hh], ("v", 2, g))

        @pl.when((y >= 2) & (hh >= h))
        def _():
            attend(2, hh, False)

    left, right = y * 4 + at[LEFT], y * 4 + at[RIGHT]
    far = y * 4 + at[FAR]
    arrived(w_at(left), "wz-left")
    send(w_at(left, 0), w_at(left, 0), "wz-far-0", zr)
    arrived(w_at(right), "wz-right")
    send(w_at(right, 1), w_at(right, 1), "wz-far-1", zl)
    send(v_own, vbuf.at[0, h], ("v", 0, LEFT), zr)
    send(v_own, vbuf.at[0, h], ("v", 0, RIGHT), zl)

    own_k.wait()
    own_v.wait()
    own_w.wait()
    attend(0, h, True)
    next_row(OWN)

    def w_row(row, half=None):
        if half is None:
            return wbuf.at[pl.ds(row * 4, 4), pl.ds(piece, 16), :]
        return wbuf.at[pl.ds(row * 4, 4), pl.ds(piece, 16), pl.ds(half * 512, 512)]

    arrived(w_at(far, 0), "wz-far-0")
    arrived(w_at(far, 1), "wz-far-1")
    send(w_row(y), w_row(y), "wy-down", yu)
    send(w_row(y), w_row(y), "wy-up", yd)
    last_row(OWN)
    below, above = (y + 3) % 4, (y + 1) % 4
    across = (y + 2) % 4
    arrived(w_row(below), "wy-down")
    send(w_row(below, 0), w_row(below, 0), "wy-far-0", yu)
    arrived(w_row(above), "wy-up")
    send(w_row(above, 1), w_row(above, 1), "wy-far-1", yd)
    arrived(w_row(across, 0), "wy-far-0")
    arrived(w_row(across, 1), "wy-far-1")

    def w_x(xx, half=None):
        rows = pl.ds(pl.multiple_of(xx * 32 + core * 16, 16), 16)
        if half is None:
            return wbuf.at[:, rows, :]
        return wbuf.at[pl.ds(half * 8, 8), rows, :]

    def w_twin(xx):
        return wbuf.at[:, pl.ds(pl.multiple_of(xx * 32 + (1 - core) * 16, 16), 16), :]

    xb, xa, xo = (x + 3) % 4, (x + 1) % 4, (x + 2) % 4
    send(w_x(x), w_x(x), "wx-down", xu)
    send(w_x(x), w_x(x), "wx-up", xd)
    send(w_x(x), w_x(x), "wc-own", twin)

    same_row(LEFT)
    same_row(RIGHT)
    next_row(LEFT)
    next_row(RIGHT)
    arrived(w_x(xb), "wx-down")
    send(w_x(xb, 0), w_x(xb, 0), "wx-far-0", xu)
    send(w_x(xb), w_x(xb), "wc-down", twin)
    arrived(w_x(xa), "wx-up")
    send(w_x(xa, 1), w_x(xa, 1), "wx-far-1", xd)
    send(w_x(xa), w_x(xa), "wc-up", twin)
    same_row(FAR)
    last_row(LEFT)
    last_row(RIGHT)
    next_row(FAR)
    arrived(w_x(xo, 0), "wx-far-0")
    arrived(w_x(xo, 1), "wx-far-1")
    send(w_x(xo), w_x(xo), "wc-far", twin)
    last_row(FAR)

    for head in range(HQ):
        b, part = head // PER, (head % PER) * TOK
        mixed = acc_s[b, :, part:part + TOK] / l_s[b, :, part:part + TOK]
        att_s[:, head * HD:(head + 1) * HD] = mixed.T.astype(jnp.bfloat16)
    arrived(w_twin(x), "wc-own")
    arrived(w_twin(xb), "wc-down")
    arrived(w_twin(xa), "wc-up")
    arrived(w_twin(xo), "wc-far")

    def project(n, carry):
        cols = pl.ds(pl.multiple_of(n * 256, 256), 256)
        weight = wbuf[:, :, cols].reshape(HQ * HD, 256)
        hidden_out[:, cols] = residual[:, cols].astype(jnp.float32) + jnp.dot(
            att_s[...], weight, preferred_element_type=jnp.float32
        )
        return carry

    lax.fori_loop(0, WIDTH // 256, project, 0)
    hidden = hidden_out[...]
    mean = jnp.mean(hidden * hidden, axis=1, keepdims=True)
    normed = (hidden * lax.rsqrt(mean + 1e-06) * gain[...]).astype(jnp.bfloat16)

    owner = lax.broadcasted_iota(jnp.int32, (OWNERS, TOK), 0)
    hit = jnp.zeros((OWNERS, TOK), jnp.float32)
    mix = jnp.zeros((OWNERS, TOK), jnp.float32)
    for k in range(TOP):
        match = owner == ids[k:k + 1, :]
        hit = jnp.where(match, 1.0, hit)
        mix = jnp.where(match, weights[k:k + 1, :], mix)
    earlier = lax.broadcasted_iota(jnp.int32, (TOK, TOK), 0) < lax.broadcasted_iota(
        jnp.int32, (TOK, TOK), 1
    )
    rank = jnp.dot(
        hit.astype(jnp.bfloat16), jnp.where(earlier, 1.0, 0.0).astype(jnp.bfloat16),
        preferred_element_type=jnp.float32,
    )
    slot = lax.broadcasted_iota(jnp.int32, (CAP, TOK), 0).astype(jnp.float32)
    places, mixes = [], []
    for owner_index in range(OWNERS):
        one = slice(owner_index, owner_index + 1)
        here = (rank[one] == slot) & (hit[one] > 0.5)
        places.append(jnp.where(here, 1.0, 0.0))
        mixes.append(jnp.where(here, mix[one], 0.0))
    place = jnp.concatenate(places, axis=0).astype(jnp.bfloat16)
    rows_out[...] = jnp.dot(place, normed, preferred_element_type=jnp.float32).astype(jnp.bfloat16)
    mixed = jnp.concatenate(mixes, axis=0)
    high = mixed.astype(jnp.bfloat16)
    hi_out[...] = high
    lo_out[...] = (mixed - high.astype(jnp.float32)).astype(jnp.bfloat16)

    for copy in sends:
        copy.wait_send()


def attend_call(queries, segments, residual, gain, ids, weights, keys, values, out_weight):
    vmem = pl.BlockSpec(memory_space=pltpu.VMEM)
    hbm = pl.BlockSpec(memory_space=pl.ANY)
    return pl.pallas_call(
        attend_kernel,
        out_shape=(
            jax.ShapeDtypeStruct((TOK, WIDTH), jnp.float32),
            jax.ShapeDtypeStruct((SLOTS, WIDTH), jnp.bfloat16),
            jax.ShapeDtypeStruct((SLOTS, TOK), jnp.bfloat16),
            jax.ShapeDtypeStruct((SLOTS, TOK), jnp.bfloat16),
        ),
        in_specs=[vmem] * 6 + [hbm] * 3,
        out_specs=(vmem,) * 4,
        scratch_shapes=[
            pltpu.VMEM((3, 4, TOK, KVH * HD), jnp.bfloat16),
            pltpu.VMEM((3, 4, TOK, KVH * HD), jnp.bfloat16),
            pltpu.VMEM((4, TOK, KVH * HD), jnp.bfloat16),
            pltpu.VMEM((HQ, HD, WIDTH), jnp.bfloat16),
            pltpu.VMEM((BLOCKS, LANES, HD), jnp.bfloat16),
            pltpu.VMEM((BLOCKS, 1, LANES), jnp.float32),
            pltpu.VMEM((BLOCKS, 1, LANES), jnp.float32),
            pltpu.VMEM((BLOCKS, HD, LANES), jnp.float32),
            pltpu.VMEM((1, LANES), jnp.int32),
            pltpu.VMEM((1, LANES), jnp.int32),
            pltpu.VMEM((TOK, HQ * HD), jnp.bfloat16),
            pltpu.SemaphoreType.DMA((48,)),
            pltpu.SemaphoreType.DMA((48,)),
            pltpu.SemaphoreType.DMA((3,)),
        ],
        compiler_params=pltpu.CompilerParams(
            collective_id=0, has_side_effects=True, vmem_limit_bytes=48 << 20
        ),
    )(queries, segments, residual, gain, ids, weights, keys, values, out_weight)


def per_device(
    queries, keys, values, segments, residual, out_weight, gain, expert_ids, route_weights,
    w_gate, w_up, w_down,
):
    hidden, rows, high, low = attend_call(
        queries[0],
        segments,
        residual[0],
        gain[None],
        expert_ids[0].T,
        route_weights[0].T,
        keys,
        values,
        out_weight,
    )
    outgoing = rows.reshape(OWNERS, CAP, WIDTH)
    arrived = lax.all_to_all(outgoing, "exp", split_axis=0, concat_axis=0, tiled=True)
    flat_rows = arrived.reshape(SLOTS, WIDTH)
    gate_part = jnp.dot(flat_rows, w_gate[0], preferred_element_type=jnp.float32)
    up_part = jnp.dot(flat_rows, w_up[0], preferred_element_type=jnp.float32)
    expert_hidden = (jax.nn.silu(gate_part) * up_part).astype(jnp.bfloat16)
    expert_out = jnp.dot(expert_hidden, w_down[0], preferred_element_type=jnp.float32).astype(
        jnp.bfloat16
    )
    returned = lax.all_to_all(
        expert_out.reshape(OWNERS, CAP, WIDTH), "exp", split_axis=0, concat_axis=0, tiled=True
    ).reshape(SLOTS, WIDTH)
    moe_sum = lax.dot_general(
        high, returned, (((0,), (0,)), ((), ())), preferred_element_type=jnp.float32
    ) + lax.dot_general(
        low, returned, (((0,), (0,)), ((), ())), preferred_element_type=jnp.float32
    )
    return (hidden + moe_sum).astype(jnp.bfloat16)[None]


def solution(mesh):
    return jax.shard_map(
        per_device,
        mesh=mesh,
        in_specs=(
            P(("dp", "exp"), "ctx", None),
            P(("dp", "exp"), "ctx", None),
            P(("dp", "exp"), "ctx", None),
            P(("dp", "exp"), None),
            P(("dp", "exp"), "ctx", None),
            P("ctx", None),
            P(),
            P(("dp", "exp"), "ctx", None),
            P(("dp", "exp"), "ctx", None),
            P("exp", None, None),
            P("exp", None, None),
            P("exp", None, None),
        ),
        out_specs=P(("dp", "exp"), "ctx", None),
        check_vma=False,
    )
```

time: 395 us -> 133 us (0.34)
  waiting for transfers between devices: 196 us -> 0 us
  Pallas kernels: 0 us -> 67.2 us
  matrix products: 58.6 us -> 5.23 us
  other arithmetic: 44.6 us -> 0 us
  local copies, waits for them, and re-layouts: 39.7 us -> 7.73 us
  blocking collectives: 25.8 us -> 51.3 us
  between operations: 13.4 us -> 0.04 us
  loops' own time: 11.2 us -> 0 us
    all_gather x3 -> x0, waiting for transfers between devices: 173 us -> none  [the longest x1 81.9 us: per_device(): key_piece = lax.all_gather(keys, 'ctx', axis=1, tiled=True)]
    pallas_call x0 -> x1, Pallas kernels: none -> 67.2 us  [attend_call(): pl.pallas_call(attend_kernel, out_shape=(jax.ShapeDtypeStruct((TOK, WIDTH...]
    dot_general x15 -> x2, matrix products: 54.9 us -> 1.54 us  [the longest x1 1.15 us: per_device(): lax.dot_general(low, returned, (((0,), (0,)), ((), ())), preferred_elemen...]
    reduce_sum x7 -> x0, other arithmetic: 26 us -> none  [the longest x6 26 us: attend_block(): new_sum = run_sum * correction + jnp.sum(expo, axis=-1)]
    all_to_all x0 -> x1, blocking collectives: none -> 24.3 us  [per_device(): lax.all_to_all(expert_out.reshape(OWNERS, CAP, WIDTH), 'exp', split_axis=...]
    dynamic_slice x19 -> x0, local copies, waits for them, and re-layouts: 21.4 us -> none  [the longest x12 15.4 us: per_device(): lax.scan(attend_block, running, (key_blocks, value_blocks, blk_starts))]
    all_to_all x1 -> x0, waiting for transfers between devices: 20.9 us -> none  [per_device(): lax.all_to_all(expert_out.reshape(owners, item_count, model_width), 'exp'...]
    another operation x1 -> x0, loops' own time: 11.2 us -> none  [per_device(): lax.scan(attend_block, running, (key_blocks, value_blocks, blk_starts))]
  transfers between devices with their start and end apart: 4 -> 0, of which waited for: 4 -> 0; matrix products, arithmetic and copies ran while one was open for 31% -> 0% of each run, Pallas kernels for 0% -> 0%
where the time goes in v1:
time: 133 us; the launch traced here: 132 us
  Pallas kernels  67.2 us (51%)
  blocking collectives  51.3 us (39%)
  local copies, waits for them, and re-layouts  7.73 us (6%)
  matrix products  5.23 us (4%)
    pallas_call x1, Pallas kernels, attend_call(): pl.pallas_call(attend_kernel, out_shape=(jax.ShapeDtypeStruct((TOK, WIDTH...  67.2 us
    all_to_all x1, blocking collectives, per_device(): lax.all_to_all(outgoing, 'exp', split_axis=0, concat_axis=0, tiled=True)  27.1 us
    all_to_all x1, blocking collectives, per_device(): lax.all_to_all(expert_out.reshape(OWNERS, CAP, WIDTH), 'exp', split_axis=...  24.3 us
    unnamed x22, local copies, waits for them, and re-layouts  7.73 us

profile of v1, /device:TPU:1, one launch (start us, length us, event | category | flops | bytes accessed | tf_op | source)
XLA Modules:
  0.0 131.6 jit_solution(568647918562313530)
XLA Ops:
  0.0 0.0 copy-start
  0.0 0.0 copy-start.1
  0.0 1.2 copy-done.1
  1.2 0.0 copy-start.2
  1.2 1.0 copy-done.2
  2.2 0.0 copy-start.3
  2.2 0.9 copy-done.3
  3.2 0.0 copy-start.4
  3.2 0.9 copy-done.4
  4.1 0.9 copy-done.5
  4.9 0.7 copy-done.6
  5.7 0.7 copy-done.7
  6.4 0.7 copy-done.8
  7.0 0.7 copy-done.9
  7.7 67.2 %shard_map.118 = (f32[192,1024]{1,0:T(8,128)S(1)}, bf16[384,1024]{1,0:T(8,128)(2,1)S(1)}, bf16[384,192]{1,0:T(8,128)(2,1)S(1)}, bf16[384,192]{1,0:T(8,128)(2,1)S(1)}) custom-call(bf16[192,2048]{1,0:T(8,128)(2,1)S(1)} %bitcast.31, s32[1,3072]{1,0:T(1,128)S(1)} %copy-done.6, bf16[192,1024]{1,0:T(8,128)(2,1)S(1)} %bitcast.33, f32[1,1024]{1,0:T(1,128)S(1)} %bitcast.36, ...), custom_call_target="tpu_custom_call" | custom-call | tf_op jit(solution)/shard_map/pallas_call | solution.py:310
  75.0 0.0 copy-start.10
  75.0 27.1 %all_to_all.10 = bf16[16,24,1024]{2,1,0:T(8,128)(2,1)S(1)} all-to-all(bf16[16,24,1024]{2,1,0:T(8,128)(2,1)S(1)} %bitcast.32), channel_id=1, replica_groups=mesh['ctx'=16,'exp'=16,'dp'=2] {'exp'}, dimensions={0} | all-to-all | bytes 1572864 | tf_op jit(solution)/shard_map/all_to_all | solution.py:358
  102.1 0.0 copy-done.10
  102.1 1.4 %fusion.7 = f32[384,384]{1,0:T(8,128)} fusion(bf16[384,1024]{1,0:T(8,128)(2,1)S(1)} %bitcast.39, bf16[1,1024,384]{2,1,0:T(8,128)(2,1)S(1)} %copy-done.10), kind=kOutput, calls=%fused_computation.9 | convolution fusion | flops 301989888 | bytes 2162688 | tf_op jit(solution)/shard_map/dot_general | solution.py:360
  103.5 0.0 copy-done
  103.5 2.3 %convolution_convert_fusion = bf16[384,1024]{1,0:T(8,128)(2,1)S(1)} fusion(bf16[384,1024]{1,0:T(8,128)(2,1)S(1)} %bitcast.40, bf16[1,384,1024]{2,1,0:T(8,128)(2,1)S(1)} %copy-done, bf16[1,1024,384]{2,1,0:T(8,128)(2,1)} %param.22, f32[384,384]{1,0:T(8,128)} %fusion.7), kind=kOutput, calls=%fused_computation | convolution fusion | flops 605257728 | bytes 3735552 | tf_op jit(solution)/shard_map/dot_general | solution.py:363
  105.8 24.3 %all_to_all.11 = bf16[16,24,1024]{2,1,0:T(8,128)(2,1)S(1)} all-to-all(bf16[16,24,1024]{2,1,0:T(8,128)(2,1)S(1)} %bitcast.41), channel_id=1, replica_groups=mesh['ctx'=16,'exp'=16,'dp'=2] {'exp'}, dimensions={0} | all-to-all | bytes 1572864 | tf_op jit(solution)/shard_map/all_to_all | solution.py:366
  130.1 0.4 fusion.16
  130.5 1.1 fusion.3
  (5 shorter events, 0.0 us)
Async XLA Ops:
  0.0 103.5 %copy-start = (bf16[1,384,1024]{2,1,0:T(8,128)(2,1)S(1)}, bf16[1,384,1024]{2,1,0:T(8,128)(2,1)}, u32[]{:S(2)}) copy-start(bf16[1,384,1024]{2,1,0:T(8,128)(2,1)} %param.23) | copy-start | bytes 2359300
  0.0 1.2 copy-start.1
  1.2 1.0 copy-start.2
  2.2 0.9 copy-start.3
  3.2 0.9 copy-start.4
  4.1 0.9 copy-start.5
  4.9 0.7 copy-start.6
  5.7 0.7 copy-start.7
  6.3 0.7 copy-start.8
  7.0 0.7 copy-start.9
  75.0 27.1 %copy-start.10 = (bf16[1,1024,384]{2,1,0:T(8,128)(2,1)S(1)}, bf16[1,1024,384]{2,1,0:T(8,128)(2,1)}, u32[]{:S(2)}) copy-start(bf16[1,1024,384]{2,1,0:T(8,128)(2,1)} %param.21) | copy-start | bytes 2359300

commit v2 on v1

--- a/solution.py
+++ b/solution.py
@@ -14,6 +14,7 @@
 CAP = 24
 TOK = 192
 WIDTH = 1024
+FFE = 384
 OWNERS = 16
 SLOTS = OWNERS * CAP
 PER = 4
@@ -25,10 +26,13 @@
 OWN, LEFT, RIGHT, FAR = range(4)
 
 
-def attend_kernel(
-    queries, segs, residual, gain, ids, weights, keys_hbm, values_hbm, w_hbm,
-    hidden_out, rows_out, hi_out, lo_out,
+def layer_kernel(
+    queries_hbm, segs_hbm, residual_hbm, gain_hbm, ids_hbm, weights_hbm, keys_hbm, values_hbm,
+    w_hbm, gate_hbm, up_hbm, down_hbm,
+    layer_out,
+    segs, residual, gain, ids, weights, gate_up, down,
     kbuf, vbuf, vtransit, wbuf, q_s, m_s, l_s, acc_s, start_s, qpos_s, att_s,
+    hidden_s, place_s, mix_s, rows_s, inbox, outbox, back,
     send_sems, recv_sems, local_sems,
 ):
     c = lax.axis_index("ctx")
@@ -40,7 +44,13 @@
     yu, yd = {"ctx": ((y + 1) % 4) * 4 + h}, {"ctx": ((y + 3) % 4) * 4 + h}
     xu, xd = {"exp": ((x + 1) % 4) * 4 + z}, {"exp": ((x + 3) % 4) * 4 + z}
     twin = {"dp": 1 - core}
-    partners = (zr, zl, yu, yd, xu, xd, twin)
+    mates = (z, z + 1 - 2 * (z % 2), (z + 2) % 4, 3 - z)
+    peers = [(b, dx) for b in range(4) for dx in (0, 1, 3, 2)]
+
+    def peer(b, dx):
+        return ((x + dx) % 4) * 4 + mates[b]
+
+    partners = (zr, zl, yu, yd, twin) + tuple({"exp": peer(*p)} for p in peers if p != (0, 0))
     at = (h, (h + 3) % 4, (h + 1) % 4, (h + 2) % 4)
 
     sends = []
@@ -71,9 +81,37 @@
     piece = pl.multiple_of(x * 32 + core * 16, 16)
     w_own = w_hbm.at[pl.ds(piece, 16), :]
     own_w = pltpu.make_async_copy(w_own, wbuf.at[c, pl.ds(piece, 16), :], local_sems.at[2])
+    loads = [
+        pltpu.make_async_copy(
+            queries_hbm.at[0, :, pl.ds(head * HD, HD)],
+            q_s.at[head // PER, pl.ds((head % PER) * TOK, TOK), :],
+            local_sems.at[3 + head],
+        )
+        for head in range(HQ)
+    ]
+    loads += [
+        pltpu.make_async_copy(src, dst, local_sems.at[3 + HQ + i])
+        for i, (src, dst) in enumerate((
+            (segs_hbm, segs),
+            (ids_hbm, ids),
+            (weights_hbm, weights),
+        ))
+    ]
+    late = [
+        pltpu.make_async_copy(src, dst, local_sems.at[6 + HQ + i])
+        for i, (src, dst) in enumerate((
+            (residual_hbm.at[0], residual),
+            (gain_hbm, gain),
+            (gate_hbm.at[0], gate_up.at[:, pl.ds(0, FFE)]),
+            (up_hbm.at[0], gate_up.at[:, pl.ds(FFE, FFE)]),
+            (down_hbm.at[0], down),
+        ))
+    ]
+    own_w.start()
     own_k.start()
     own_v.start()
-    own_w.start()
+    for load in loads:
+        load.start()
     pl.semaphore_wait(barrier, len(partners))
 
     k_own, v_own = keys_hbm.at[0], values_hbm.at[0]
@@ -91,10 +129,10 @@
     send(v_own, vbuf.at[1, h], ("v", 1, OWN), yu)
     send(v_own, vtransit.at[h], ("t", OWN), yd)
 
-    for head in range(HQ):
-        q_s[head // PER, (head % PER) * TOK:(head % PER + 1) * TOK, :] = (
-            queries[:, head * HD:(head + 1) * HD]
-        )
+    for load in late:
+        load.start()
+    for load in loads:
+        load.wait()
     line = segs[...]
     mine = jnp.zeros((1, TOK), jnp.int32)
     for slab in range(16):
@@ -106,6 +144,30 @@
     start_s[...] = jnp.concatenate([start] * PER, axis=1)
     qpos = c * TOK + lax.broadcasted_iota(jnp.int32, (1, TOK), 1)
     qpos_s[...] = jnp.concatenate([qpos] * PER, axis=1)
+
+    owner = lax.broadcasted_iota(jnp.int32, (OWNERS, TOK), 0)
+    hit = jnp.zeros((OWNERS, TOK), jnp.float32)
+    mix = jnp.zeros((OWNERS, TOK), jnp.float32)
+    for k in range(TOP):
+        match = owner == ids[k:k + 1, :]
+        hit = jnp.where(match, 1.0, hit)
+        mix = jnp.where(match, weights[k:k + 1, :], mix)
+    earlier = lax.broadcasted_iota(jnp.int32, (TOK, TOK), 0) < lax.broadcasted_iota(
+        jnp.int32, (TOK, TOK), 1
+    )
+    rank = jnp.dot(
+        hit.astype(jnp.bfloat16), jnp.where(earlier, 1.0, 0.0).astype(jnp.bfloat16),
+        preferred_element_type=jnp.float32,
+    )
+    slot = lax.broadcasted_iota(jnp.int32, (CAP, TOK), 0).astype(jnp.float32)
+    places, mixes = [], []
+    for owner_index in range(OWNERS):
+        one = slice(owner_index, owner_index + 1)
+        here = (rank[one] == slot) & (hit[one] > 0.5)
+        places.append(jnp.where(here, 1.0, 0.0))
+        mixes.append(jnp.where(here, mix[one], 0.0))
+    place_s[...] = jnp.concatenate(places, axis=0).astype(jnp.bfloat16)
+    mix_s[...] = jnp.concatenate(mixes, axis=0).reshape(OWNERS, CAP, TOK)
 
     def attend(r, hh, diagonal):
         first = ((y - r) * 4 + hh) * TOK
@@ -259,119 +321,124 @@
     arrived(w_twin(xa), "wc-up")
     arrived(w_twin(xo), "wc-far")
 
+    for load in late:
+        load.wait()
+
     def project(n, carry):
         cols = pl.ds(pl.multiple_of(n * 256, 256), 256)
         weight = wbuf[:, :, cols].reshape(HQ * HD, 256)
-        hidden_out[:, cols] = residual[:, cols].astype(jnp.float32) + jnp.dot(
+        hidden_s[:, cols] = residual[:, cols].astype(jnp.float32) + jnp.dot(
             att_s[...], weight, preferred_element_type=jnp.float32
         )
         return carry
 
     lax.fori_loop(0, WIDTH // 256, project, 0)
-    hidden = hidden_out[...]
+    hidden = hidden_s[...]
     mean = jnp.mean(hidden * hidden, axis=1, keepdims=True)
     normed = (hidden * lax.rsqrt(mean + 1e-06) * gain[...]).astype(jnp.bfloat16)
 
-    owner = lax.broadcasted_iota(jnp.int32, (OWNERS, TOK), 0)
-    hit = jnp.zeros((OWNERS, TOK), jnp.float32)
-    mix = jnp.zeros((OWNERS, TOK), jnp.float32)
-    for k in range(TOP):
-        match = owner == ids[k:k + 1, :]
-        hit = jnp.where(match, 1.0, hit)
-        mix = jnp.where(match, weights[k:k + 1, :], mix)
-    earlier = lax.broadcasted_iota(jnp.int32, (TOK, TOK), 0) < lax.broadcasted_iota(
-        jnp.int32, (TOK, TOK), 1
-    )
-    rank = jnp.dot(
-        hit.astype(jnp.bfloat16), jnp.where(earlier, 1.0, 0.0).astype(jnp.bfloat16),
-        preferred_element_type=jnp.float32,
-    )
-    slot = lax.broadcasted_iota(jnp.int32, (CAP, TOK), 0).astype(jnp.float32)
-    places, mixes = [], []
-    for owner_index in range(OWNERS):
-        one = slice(owner_index, owner_index + 1)
-        here = (rank[one] == slot) & (hit[one] > 0.5)
-        places.append(jnp.where(here, 1.0, 0.0))
-        mixes.append(jnp.where(here, mix[one], 0.0))
-    place = jnp.concatenate(places, axis=0).astype(jnp.bfloat16)
-    rows_out[...] = jnp.dot(place, normed, preferred_element_type=jnp.float32).astype(jnp.bfloat16)
-    mixed = jnp.concatenate(mixes, axis=0)
-    high = mixed.astype(jnp.bfloat16)
-    hi_out[...] = high
-    lo_out[...] = (mixed - high.astype(jnp.float32)).astype(jnp.bfloat16)
+    placed = jnp.dot(place_s[...], normed, preferred_element_type=jnp.float32)
+    rows_s[...] = placed.reshape(OWNERS, CAP, WIDTH).astype(jnp.bfloat16)
+    for b, dx in peers:
+        if (b, dx) == (0, 0):
+            inbox[e] = rows_s[e]
+        else:
+            to = peer(b, dx)
+            send(rows_s.at[to], inbox.at[e], ("out", b, (4 - dx) % 4), {"exp": to})
+
+    def four(ref, b):
+        return jnp.concatenate(
+            [ref[peer(b, dx)].astype(jnp.float32) for dx in range(4)], axis=0
+        )
+
+    for b in range(4):
+        for dx in range(4):
+            if (b, dx) != (0, 0):
+                arrived(inbox.at[peer(b, dx)], ("out", b, dx))
+        fed = jnp.dot(
+            four(inbox, b).astype(jnp.bfloat16), gate_up[...], preferred_element_type=jnp.float32
+        )
+        gated, upped = fed[:, :FFE], fed[:, FFE:]
+        inner = (gated / (1.0 + jnp.exp(-gated)) * upped).astype(jnp.bfloat16)
+        result = jnp.dot(inner, down[...], preferred_element_type=jnp.float32)
+        result = result.reshape(4, CAP, WIDTH).astype(jnp.bfloat16)
+        for dx in range(4):
+            if (b, dx) == (0, 0):
+                back[e] = result[dx]
+            else:
+                outbox[peer(b, dx)] = result[dx]
+        for dx in (0, 1, 3, 2):
+            if (b, dx) != (0, 0):
+                to = peer(b, dx)
+                send(outbox.at[to], back.at[e], ("back", b, (4 - dx) % 4), {"exp": to})
+
+    for b in range(4):
+        for dx in range(4):
+            if (b, dx) != (0, 0):
+                arrived(back.at[peer(b, dx)], ("back", b, dx))
+        mixes = four(mix_s, b)
+        high = mixes.astype(jnp.bfloat16)
+        low = (mixes - high.astype(jnp.float32)).astype(jnp.bfloat16)
+        got = four(back, b).astype(jnp.bfloat16)
+        hidden_s[...] += lax.dot_general(
+            jnp.concatenate([high, low], axis=0), jnp.concatenate([got, got], axis=0),
+            (((0,), (0,)), ((), ())), preferred_element_type=jnp.float32,
+        )
+    layer_out[...] = hidden_s[...].astype(jnp.bfloat16)
 
     for copy in sends:
         copy.wait_send()
-
-
-def attend_call(queries, segments, residual, gain, ids, weights, keys, values, out_weight):
-    vmem = pl.BlockSpec(memory_space=pltpu.VMEM)
-    hbm = pl.BlockSpec(memory_space=pl.ANY)
-    return pl.pallas_call(
-        attend_kernel,
-        out_shape=(
-            jax.ShapeDtypeStruct((TOK, WIDTH), jnp.float32),
-            jax.ShapeDtypeStruct((SLOTS, WIDTH), jnp.bfloat16),
-            jax.ShapeDtypeStruct((SLOTS, TOK), jnp.bfloat16),
-            jax.ShapeDtypeStruct((SLOTS, TOK), jnp.bfloat16),
-        ),
-        in_specs=[vmem] * 6 + [hbm] * 3,
-        out_specs=(vmem,) * 4,
-        scratch_shapes=[
-            pltpu.VMEM((3, 4, TOK, KVH * HD), jnp.bfloat16),
-            pltpu.VMEM((3, 4, TOK, KVH * HD), jnp.bfloat16),
-            pltpu.VMEM((4, TOK, KVH * HD), jnp.bfloat16),
-            pltpu.VMEM((HQ, HD, WIDTH), jnp.bfloat16),
-            pltpu.VMEM((BLOCKS, LANES, HD), jnp.bfloat16),
-            pltpu.VMEM((BLOCKS, 1, LANES), jnp.float32),
-            pltpu.VMEM((BLOCKS, 1, LANES), jnp.float32),
-            pltpu.VMEM((BLOCKS, HD, LANES), jnp.float32),
-            pltpu.VMEM((1, LANES), jnp.int32),
-            pltpu.VMEM((1, LANES), jnp.int32),
-            pltpu.VMEM((TOK, HQ * HD), jnp.bfloat16),
-            pltpu.SemaphoreType.DMA((48,)),
-            pltpu.SemaphoreType.DMA((48,)),
-            pltpu.SemaphoreType.DMA((3,)),
-        ],
-        compiler_params=pltpu.CompilerParams(
-            collective_id=0, has_side_effects=True, vmem_limit_bytes=48 << 20
-        ),
-    )(queries, segments, residual, gain, ids, weights, keys, values, out_weight)
 
 
 def per_device(
     queries, keys, values, segments, residual, out_weight, gain, expert_ids, route_weights,
     w_gate, w_up, w_down,
 ):
-    hidden, rows, high, low = attend_call(
-        queries[0],
-        segments,
-        residual[0],
-        gain[None],
-        expert_ids[0].T,
-        route_weights[0].T,
-        keys,
-        values,
-        out_weight,
+    hbm = pl.BlockSpec(memory_space=pl.ANY)
+    bf16, f32 = jnp.bfloat16, jnp.float32
+    result = pl.pallas_call(
+        layer_kernel,
+        out_shape=jax.ShapeDtypeStruct((TOK, WIDTH), bf16),
+        in_specs=[hbm] * 12,
+        out_specs=pl.BlockSpec(memory_space=pltpu.VMEM),
+        scratch_shapes=[
+            pltpu.VMEM((1, 16 * TOK), jnp.int32),
+            pltpu.VMEM((TOK, WIDTH), bf16),
+            pltpu.VMEM((1, WIDTH), f32),
+            pltpu.VMEM((TOP, TOK), jnp.int32),
+            pltpu.VMEM((TOP, TOK), f32),
+            pltpu.VMEM((WIDTH, 2 * FFE), bf16),
+            pltpu.VMEM((FFE, WIDTH), bf16),
+            pltpu.VMEM((3, 4, TOK, KVH * HD), bf16),
+            pltpu.VMEM((3, 4, TOK, KVH * HD), bf16),
+            pltpu.VMEM((4, TOK, KVH * HD), bf16),
+            pltpu.VMEM((HQ, HD, WIDTH), bf16),
+            pltpu.VMEM((BLOCKS, LANES, HD), bf16),
+            pltpu.VMEM((BLOCKS, 1, LANES), f32),
+            pltpu.VMEM((BLOCKS, 1, LANES), f32),
+            pltpu.VMEM((BLOCKS, HD, LANES), f32),
+            pltpu.VMEM((1, LANES), jnp.int32),
+            pltpu.VMEM((1, LANES), jnp.int32),
+            pltpu.VMEM((TOK, HQ * HD), bf16),
+            pltpu.VMEM((TOK, WIDTH), f32),
+            pltpu.VMEM((SLOTS, TOK), bf16),
+            pltpu.VMEM((OWNERS, CAP, TOK), f32),
+            pltpu.VMEM((OWNERS, CAP, WIDTH), bf16),
+            pltpu.VMEM((OWNERS, CAP, WIDTH), bf16),
+            pltpu.VMEM((OWNERS, CAP, WIDTH), bf16),
+            pltpu.VMEM((OWNERS, CAP, WIDTH), bf16),
+            pltpu.SemaphoreType.DMA((80,)),
+            pltpu.SemaphoreType.DMA((80,)),
+            pltpu.SemaphoreType.DMA((32,)),
+        ],
+        compiler_params=pltpu.CompilerParams(
+            collective_id=0, has_side_effects=True, vmem_limit_bytes=67043328
+        ),
+    )(
+        queries, segments, residual, gain[None], expert_ids[0].T, route_weights[0].T, keys, values,
+        out_weight, w_gate, w_up, w_down,
     )
-    outgoing = rows.reshape(OWNERS, CAP, WIDTH)
-    arrived = lax.all_to_all(outgoing, "exp", split_axis=0, concat_axis=0, tiled=True)
-    flat_rows = arrived.reshape(SLOTS, WIDTH)
-    gate_part = jnp.dot(flat_rows, w_gate[0], preferred_element_type=jnp.float32)
-    up_part = jnp.dot(flat_rows, w_up[0], preferred_element_type=jnp.float32)
-    expert_hidden = (jax.nn.silu(gate_part) * up_part).astype(jnp.bfloat16)
-    expert_out = jnp.dot(expert_hidden, w_down[0], preferred_element_type=jnp.float32).astype(
-        jnp.bfloat16
-    )
-    returned = lax.all_to_all(
-        expert_out.reshape(OWNERS, CAP, WIDTH), "exp", split_axis=0, concat_axis=0, tiled=True
-    ).reshape(SLOTS, WIDTH)
-    moe_sum = lax.dot_general(
-        high, returned, (((0,), (0,)), ((), ())), preferred_element_type=jnp.float32
-    ) + lax.dot_general(
-        low, returned, (((0,), (0,)), ((), ())), preferred_element_type=jnp.float32
-    )
-    return (hidden + moe_sum).astype(jnp.bfloat16)[None]
+    return result[None]
 
 
 def solution(mesh):

time: 133 us -> 107 us (0.80)
  the two profiles are of different devices: /device:TPU:1 before, /device:TPU:41 now
where the time goes in v2:
time: 107 us
  Pallas kernels  105 us (98%)
  local copies, waits for them, and re-layouts  1.77 us (2%)
    pallas_call x1, Pallas kernels, per_device(): pl.pallas_call(layer_kernel, out_shape=jax.ShapeDtypeStruct((TOK, WIDTH),...  105 us

profile of v2, /device:TPU:41, one launch (start us, length us, event | category | flops | bytes accessed | tf_op | source)
XLA Modules:
  0.0 106.5 jit_solution(5268310458948155245)
XLA Ops:
  0.0 104.7 %shard_map.118 = bf16[192,1024]{1,0:T(8,128)(2,1)} custom-call(bf16[1,192,2048]{2,1,0:T(8,128)(2,1)} %queries_hbm.1, s32[1,3072]{1,0:T(1,128)} %segs_hbm.1, bf16[1,192,1024]{2,1,0:T(8,128)(2,1)} %residual_hbm.1, f32[1,1024]{1,0:T(1,128)} %bitcast.11, s32[8,192]{1,0:T(8,128)} %bitcast.9, f32[8,192]{1,0:T(8,128)} %bitcast.10, bf16[1,192,256]{2,1,0:T(8,128)(2,1)} %keys_hbm.1, ...), custom_call_target="tpu_custom_call" | custom-call | tf_op jit(solution)/shard_map/pallas_call | solution.py:399
  104.8 1.8 %copy.14 = bf16[1,192,1024]{2,1,0:T(8,128)(2,1)} copy(bf16[1,192,1024]{2,1,0:T(8,128)(2,1)} %bitcast.8) | data formatting | bytes 786432

commit v3 on v2

--- a/solution.py
+++ b/solution.py
@@ -123,8 +123,6 @@
 
     send(w_own, w_at(c), "wz-left", zr)
     send(w_own, w_at(c), "wz-right", zl)
-    send(k_own, kbuf.at[0, h], ("k", 0, LEFT), zr)
-    send(k_own, kbuf.at[0, h], ("k", 0, RIGHT), zl)
     send(k_own, kbuf.at[1, h], ("k", 1, OWN), yu)
     send(v_own, vbuf.at[1, h], ("v", 1, OWN), yu)
     send(v_own, vtransit.at[h], ("t", OWN), yd)
@@ -210,15 +208,24 @@
 
     def same_row(g):
         hh = at[g]
-        arrived(kbuf.at[0, hh], ("k", 0, g))
-        if g == LEFT:
-            send(kbuf.at[0, hh], kbuf.at[0, hh], ("k", 0, FAR), zr)
-        send(kbuf.at[0, hh], kbuf.at[1, hh], ("k", 1, g), yu)
-        arrived(vbuf.at[0, hh], ("v", 0, g))
-        if g == RIGHT:
-            send(vbuf.at[0, hh], vbuf.at[0, hh], ("v", 0, FAR), zl)
-        send(vbuf.at[0, hh], vbuf.at[1, hh], ("v", 1, g), yu)
-        send(vbuf.at[0, hh], vtransit.at[hh], ("t", g), yd)
+
+        def k_part():
+            arrived(kbuf.at[0, hh], ("k", 0, g))
+            if g == LEFT:
+                send(kbuf.at[0, hh], kbuf.at[0, hh], ("k", 0, FAR), zr)
+            send(kbuf.at[0, hh], kbuf.at[1, hh], ("k", 1, g), yu)
+
+        def v_part():
+            arrived(vbuf.at[0, hh], ("v", 0, g))
+            if g == RIGHT:
+                send(vbuf.at[0, hh], vbuf.at[0, hh], ("v", 0, FAR), zl)
+            send(vbuf.at[0, hh], vtransit.at[hh], ("t", g), yd)
+            send(vbuf.at[0, hh], vbuf.at[1, hh], ("v", 1, g), yu)
+
+        return k_part, v_part
+
+    def same_attend(g):
+        hh = at[g]
 
         @pl.when(hh < h)
         def _():
@@ -251,8 +258,10 @@
     send(w_at(left, 0), w_at(left, 0), "wz-far-0", zr)
     arrived(w_at(right), "wz-right")
     send(w_at(right, 1), w_at(right, 1), "wz-far-1", zl)
+    send(k_own, kbuf.at[0, h], ("k", 0, LEFT), zr)
+    send(v_own, vbuf.at[0, h], ("v", 0, RIGHT), zl)
     send(v_own, vbuf.at[0, h], ("v", 0, LEFT), zr)
-    send(v_own, vbuf.at[0, h], ("v", 0, RIGHT), zl)
+    send(k_own, kbuf.at[0, h], ("k", 0, RIGHT), zl)
 
     own_k.wait()
     own_v.wait()
@@ -293,8 +302,14 @@
     send(w_x(x), w_x(x), "wx-up", xd)
     send(w_x(x), w_x(x), "wc-own", twin)
 
-    same_row(LEFT)
-    same_row(RIGHT)
+    left_k, left_v = same_row(LEFT)
+    right_k, right_v = same_row(RIGHT)
+    left_k()
+    right_v()
+    left_v()
+    right_k()
+    same_attend(LEFT)
+    same_attend(RIGHT)
     next_row(LEFT)
     next_row(RIGHT)
     arrived(w_x(xb), "wx-down")
@@ -303,7 +318,10 @@
     arrived(w_x(xa), "wx-up")
     send(w_x(xa, 1), w_x(xa, 1), "wx-far-1", xd)
     send(w_x(xa), w_x(xa), "wc-up", twin)
-    same_row(FAR)
+    far_k, far_v = same_row(FAR)
+    far_k()
+    far_v()
+    same_attend(FAR)
     last_row(LEFT)
     last_row(RIGHT)
     next_row(FAR)

time: 107 us -> 104 us (0.972)
  the two profiles are of different devices: /device:TPU:41 before, /device:TPU:48 now
where the time goes in v3:
time: 104 us
  Pallas kernels  103 us (99%)
  local copies, waits for them, and re-layouts  1.77 us (2%)
    pallas_call x1, Pallas kernels, per_device(): pl.pallas_call(layer_kernel, out_shape=jax.ShapeDtypeStruct((TOK, WIDTH),...  103 us

profile of v3, /device:TPU:48, one launch (start us, length us, event | category | flops | bytes accessed | tf_op | source)
XLA Modules:
  0.0 104.3 jit_solution(16443249552623516483)
XLA Ops:
  0.0 102.5 %shard_map.118 = bf16[192,1024]{1,0:T(8,128)(2,1)} custom-call(bf16[1,192,2048]{2,1,0:T(8,128)(2,1)} %queries_hbm.1, s32[1,3072]{1,0:T(1,128)} %segs_hbm.1, bf16[1,192,1024]{2,1,0:T(8,128)(2,1)} %residual_hbm.1, f32[1,1024]{1,0:T(1,128)} %bitcast.11, s32[8,192]{1,0:T(8,128)} %bitcast.9, f32[8,192]{1,0:T(8,128)} %bitcast.10, bf16[1,192,256]{2,1,0:T(8,128)(2,1)} %keys_hbm.1, ...), custom_call_target="tpu_custom_call" | custom-call | tf_op jit(solution)/shard_map/pallas_call | solution.py:417
  102.5 1.8 %copy.14 = bf16[1,192,1024]{2,1,0:T(8,128)(2,1)} copy(bf16[1,192,1024]{2,1,0:T(8,128)(2,1)} %bitcast.8) | data formatting | bytes 786432
